TPU v7x, 128 devices: a whole 4x4x4 slice. The times are simulated.
128 devices in a mesh: dp: 8 (over z, core), mp: 16 (over x, y).
Axes of the slice: x: 4, y: 4, z: 4, core: 2. Of those that a mesh axis runs over, the one named last changes fastest.
Arguments:
- tokens: bfloat16 [8192, 4096], P('dp', 'mp'), parts along dimension 0, may hold values from -6 to 6
- cotangent: bfloat16 [8192, 4096], P('dp', 'mp'), parts along dimension 0, may hold values from -6 to 6
- offsets: int32 [64], P('dp'), parts along dimension 0, may hold values from 0 to 960, as said below
- w_gate: bfloat16 [4096, 14336], P(None, 'mp'), may hold values from -0.09375 to 0.09375
- w_up: bfloat16 [4096, 14336], P(None, 'mp'), may hold values from -0.09375 to 0.09375
- w_down: bfloat16 [14336, 4096], P('mp'), may hold values from -0.046875 to 0.046875
- feature_proj: bfloat16 [4096, 192], replicated, may hold values from -0.09375 to 0.09375
- hidden_proj: bfloat16 [14336, 192], P('mp'), may hold values from -0.046875 to 0.046875
Outputs:
- input_grad: bfloat16 [4096, 4096], P(('dp', 'mp')), parts along dimension 0
- projected_grads: float32 [3, 64, 64, 64], P(None, 'dp'), parts along dimension 1
There are 8 independent parts, one for each index of `dp`. A program takes and returns all parts, laid end to end along the dimension named above; an argument that names none is the same for every part. Nothing has to cross between parts.
Inputs may be any that keep to these rules, and one draw needn't show every extreme that they name: `offsets`: spans lie inside the batch and may intersect; in every draw some span starts at 0 and some at 960.
All inputs are finite; a program needn't handle non-finite values.
Results may differ from a plain program's by a relative error of at most 0.0049.
Values may be sent and summed in bfloat16 or wider, within the bound.
No kernel may reach another device: no remote copies, remote signals or barrier semaphores. Data moves between devices by JAX's collectives and lax.ppermute only.
A program may use at most 128 MiB of HBM per device.

v0:
```python
import jax
import jax.numpy as jnp
from jax import lax
from jax.sharding import PartitionSpec as P

RANK = 64
SPAN_LEN = 64


def per_device(tokens, cotangent, offsets, w_gate, w_up, w_down, feature_proj, hidden_proj):
    positions = (offsets[:, None] + jnp.arange(SPAN_LEN, dtype=jnp.int32)[None, :]).reshape(-1)
    span_rows = positions.shape[0]
    span_x = jnp.take(lax.all_gather(tokens, "mp", axis=1, tiled=True), positions, axis=0)
    span_g = jnp.take(lax.all_gather(cotangent, "mp", axis=1, tiled=True), positions, axis=0)
    sums = (
        jnp.dot(span_x, w_gate, preferred_element_type=jnp.float32),
        jnp.dot(span_x, w_up, preferred_element_type=jnp.float32),
        jnp.einsum("td,fd->tf", span_g, w_down, preferred_element_type=jnp.float32),
        jnp.dot(span_x, feature_proj, preferred_element_type=jnp.float32),
        jnp.dot(span_g, feature_proj, preferred_element_type=jnp.float32),
    )
    pre_gate, pre_up, grad_hidden, feat_x, feat_g = sums
    sigmoid_gate = jax.nn.sigmoid(pre_gate)
    activated = pre_gate * sigmoid_gate
    hidden = (activated * pre_up).astype(jnp.bfloat16)
    grad_gate = (
        grad_hidden * pre_up * sigmoid_gate * (1.0 + pre_gate * (1.0 - sigmoid_gate))
    ).astype(jnp.bfloat16)
    grad_up = (grad_hidden * activated).astype(jnp.bfloat16)
    span_count = span_rows // SPAN_LEN
    input_grad = lax.psum_scatter(
        jnp.einsum("tf,df->td", grad_gate, w_gate, preferred_element_type=jnp.float32)
        + jnp.einsum("tf,df->td", grad_up, w_up, preferred_element_type=jnp.float32),
        "mp",
        scatter_dimension=0,
        tiled=True,
    ).astype(jnp.bfloat16)
    hid_gate = jnp.dot(grad_gate, hidden_proj[:, :RANK], preferred_element_type=jnp.float32)
    hid_up = jnp.dot(grad_up, hidden_proj[:, RANK : 2 * RANK], preferred_element_type=jnp.float32)
    hid_down = jnp.dot(hidden, hidden_proj[:, 2 * RANK :], preferred_element_type=jnp.float32)
    hid_gate, hid_up, hid_down = lax.psum((hid_gate, hid_up, hid_down), "mp")

    def per_span(left, right):
        return jnp.einsum(
            "slr,slq->srq",
            left.reshape(span_count, SPAN_LEN, RANK),
            right.reshape(span_count, SPAN_LEN, RANK),
            precision=lax.Precision.HIGHEST,
        )

    projected_grads = jnp.stack(
        [
            per_span(feat_x[:, :RANK], hid_gate),
            per_span(feat_x[:, RANK : 2 * RANK], hid_up),
            per_span(hid_down, feat_g[:, 2 * RANK :]),
        ],
        axis=0,
    )
    return (input_grad, projected_grads)


def solution(mesh):
    in_specs = (
        P("dp", "mp"),
        P("dp", "mp"),
        P("dp"),
        P(None, "mp"),
        P(None, "mp"),
        P("mp", None),
        P(),
        P("mp", None),
    )
    out_specs = (P(("dp", "mp"), None), P(None, "dp", None, None))
    return jax.shard_map(
        per_device, mesh=mesh, in_specs=in_specs, out_specs=out_specs, check_vma=False
    )
```

profile of v0, /device:TPU:0, one launch (start us, length us, event | category | flops | bytes accessed | tf_op | source)
XLA Modules:
  0.0 387.4 jit_solution(1904337492347919827)
XLA Ops:
  8.7 0.7 iota_add_fusion
  9.5 80.2 %all-gather.5.cloned.1.call-done = bf16[1024,4096]{1,0:T(8,128)(2,1)} async-done(((bf16[1024,256]{1,0:T(8,128)(2,1)}), bf16[1024,4096]{1,0:T(8,128)(2,1)}) %all-gather.5.cloned.1.call-update) | async-done | bytes 8388624 | tf_op jit(solution)/shard_map/all_gather | solution.py:13
  89.7 13.0 %gather_fusion.1 = bf16[512,4096]{1,0:T(8,128)(2,1)} fusion(bf16[1024,4096]{1,0:T(8,128)(2,1)} %all-gather.5.cloned.1.call-done, s32[1024]{0:T(1024)S(1)} %pad_clamp_fusion), kind=kCustom, calls=%fused_computation.1.clone | custom fusion | bytes 8390656 | tf_op jit(solution)/shard_map/jit(_take)/gather | solution.py:13
  102.7 11.0 %fusion.18 = f32[512,896]{1,0:T(8,128)S(1)} fusion(bf16[4096,896]{1,0:T(8,128)(2,1)} %param.14, bf16[512,4096]{1,0:T(8,128)(2,1)} %gather_fusion.1, pred[512]{0:T(512)(128)(4,1)S(1)} %compare_and_fusion), kind=kOutput, calls=%fused_computation.34 | convolution fusion | flops 3760193536 | bytes 13369856 | tf_op jit(solution)/shard_map/dot_general | solution.py:17
  113.8 9.1 %fusion.17 = f32[512,896]{1,0:T(8,128)S(1)} fusion(bf16[4096,896]{1,0:T(8,128)(2,1)} %param.13, bf16[512,4096]{1,0:T(8,128)(2,1)S(1)} %copy-done, pred[512]{0:T(512)(128)(4,1)S(1)} %compare_and_fusion), kind=kOutput, calls=%fused_computation.33 | convolution fusion | flops 3760193536 | bytes 13369856 | tf_op jit(solution)/shard_map/dot_general | solution.py:16
  122.9 1.2 copy-done.3
  124.8 43.5 %all-gather.3.cloned.1.call-done = bf16[1024,4096]{1,0:T(8,128)(2,1)} async-done(((bf16[1024,256]{1,0:T(8,128)(2,1)}), bf16[1024,4096]{1,0:T(8,128)(2,1)}) %all-gather.3.cloned.1.call-update) | async-done | bytes 8388624 | tf_op jit(solution)/shard_map/all_gather | solution.py:14
  168.3 13.2 %gather_fusion = bf16[512,4096]{1,0:T(8,128)(2,1)} fusion(bf16[1024,4096]{1,0:T(8,128)(2,1)} %all-gather.3.cloned.1.call-done, s32[1024]{0:T(1024)S(1)} %pad_clamp_fusion), kind=kCustom, calls=%fused_computation.clone | custom fusion | bytes 8390656 | tf_op jit(solution)/shard_map/jit(_take)/gather | solution.py:14
  181.5 9.8 %multiply_convert_fusion.1 = (bf16[512,896]{1,0:T(8,128)(2,1)S(1)}, bf16[512,896]{1,0:T(8,128)(2,1)S(1)}) fusion(f32[512,896]{1,0:T(8,128)} %copy-done.3, f32[512,896]{1,0:T(8,128)S(1)} %fusion.18, bf16[896,4096]{1,0:T(8,128)(2,1)} %param.15, bf16[512,4096]{1,0:T(8,128)(2,1)} %gather_fusion, pred[512]{0:T(512)(128)(4,1)S(1)} %compare_and_fusion), kind=kOutput, calls=%fused_computation.6 | convolution fusion | flops 3766157312 | bytes 17039872 | tf_op jit(solution)/shard_map/td,fd->tf/dot_general | solution.py:18
  191.4 1.1 fusion.11
  192.5 9.8 %fusion.20 = f32[512,4096]{1,0:T(8,128)} fusion(bf16[512,896]{1,0:T(8,128)(2,1)S(1)} %get-tuple-element.7, bf16[4096,896]{1,0:T(8,128)(2,1)} %param.13), kind=kOutput, calls=%fused_computation.36 | convolution fusion | flops 3758096384 | bytes 16646144 | tf_op jit(solution)/shard_map/tf,df->td/dot_general | solution.py:32
  202.3 1.1 fusion.9
  203.5 0.8 copy.14
  204.3 11.3 %convolution_add_fusion = f32[512,4096]{1,0:T(8,128)} fusion(f32[512,4096]{1,0:T(8,128)} %fusion.20, bf16[512,896]{1,0:T(8,128)(2,1)S(1)} %get-tuple-element.6, bf16[4096,896]{1,0:T(8,128)(2,1)} %param.14), kind=kOutput, calls=%fused_computation.2 | convolution fusion | flops 3760193536 | bytes 25034752 | tf_op jit(solution)/shard_map/tf,df->td/dot_general | solution.py:33
  215.6 1.4 copy-done.2
  217.0 3.9 %fusion.16 = f32[512,192]{0,1:T(8,128)S(1)} fusion(bf16[4096,192]{0,1:T(8,128)(2,1)S(1)} %copy-done.2, bf16[512,4096]{1,0:T(8,128)(2,1)} %gather_fusion.1, pred[512]{0:T(512)(128)(4,1)S(1)} %compare_and_fusion), kind=kOutput, calls=%fused_computation.32 | convolution fusion | flops 807403520 | bytes 6160896 | tf_op jit(solution)/shard_map/dot_general | solution.py:19
  221.2 3.5 fusion.1
  224.7 65.8 %all-reduce.3.cloned.1.call-done = (f32[8,64,64]{1,2,0:T(8,128)}, f32[8,64,64]{2,1,0:T(8,128)}, f32[8,64,64]{2,1,0:T(8,128)}) async-done(((f32[8,64,64]{1,2,0:T(8,128)}, f32[8,64,64]{2,1,0:T(8,128)}, f32[8,64,64]{2,1,0:T(8,128)}), (f32[8,64,64]{1,2,0:T(8,128)}, f32[8,64,64]{2,1,0:T(8,128)}, f32[8,64,64]{2,1,0:T(8,128)})) %all-reduce.3.cloned.1.call-update) | async-done | bytes 393232 | tf_op jit(solution)/shard_map/psum | solution.py:41
  290.5 1.3 convolution_bitcast_fusion.2
  291.8 1.4 convolution_bitcast_fusion.1
  293.2 1.3 convolution_bitcast_fusion
  294.5 0.9 pad_maximum_fusion
  295.5 83.6 %reduce-scatter.2.cloned.1.call-done = f32[32,4096]{1,0:T(8,128)} async-done(((f32[512,4096]{1,0:T(8,128)}), f32[32,4096]{1,0:T(8,128)}) %reduce-scatter.2.cloned.1.call-update) | async-done | bytes 524304 | tf_op jit(solution)/shard_map/reduce_scatter | solution.py:31
  379.1 1.8 convert_element_type.14
  (23 shorter events, 2.7 us)
Async XLA Ops:
  7.2 82.5 %all-gather.5.cloned.1.call-start = ((), (), s32[]{:S(2)}) async-start(), calls=%async_computation.2 | async-start | bytes 8912896 | tf_op jit(solution)/shard_map/all_gather | solution.py:13
  7.9 160.4 %all-gather.3.cloned.1.call-start = ((), (), s32[]{:S(2)}) async-start(), calls=%async_computation.1 | async-start | bytes 8912896 | tf_op jit(solution)/shard_map/all_gather | solution.py:14
  8.6 281.8 %all-reduce.3.cloned.1.call-start = ((), (), s32[]{:S(2)}) async-start(), calls=%async_computation.4 | async-start | bytes 1572864 | tf_op jit(solution)/shard_map/psum | solution.py:41
  102.7 11.0 %copy-start = (bf16[512,4096]{1,0:T(8,128)(2,1)S(1)}, bf16[512,4096]{1,0:T(8,128)(2,1)}, u32[]{:S(2)}) copy-start(bf16[512,4096]{1,0:T(8,128)(2,1)} %gather_fusion.1) | copy-start | bytes 12582916
  113.8 10.4 %copy-start.1 = (bf16[896,192]{0,1:T(8,128)(2,1)S(1)}, bf16[896,192]{0,1:T(8,128)(2,1)}, u32[]{:S(2)}) copy-start(bf16[896,192]{0,1:T(8,128)(2,1)} %param.17) | copy-start | bytes 1032196
  122.9 1.3 copy-start.3
  204.3 174.8 %reduce-scatter.2.cloned.1.call-start = ((), (), s32[]{:S(2)}) async-start(), calls=%async_computation.3 | async-start | bytes 8912896 | tf_op jit(solution)/shard_map/reduce_scatter | solution.py:31
  215.6 1.4 copy-start.2
Sparse Core Ops, SparseCore 0:
  10.1 79.5 all-gather.4
  91.8 76.4 all-gather.2
  204.4 86.0 all-reduce.2
  293.8 85.2 reduce-scatter.1
where the time goes:
time: 388 us; the launch traced here: 387 us
  waiting for transfers between devices  274 us (71%)
  matrix products  65.4 us (17%)
  local copies, waits for them, and re-layouts  30.1 us (8%)
  between operations  13.9 us (4%)
    reduce_scatter x1, waiting for transfers between devices, per_device(): lax.psum_scatter(jnp.einsum('tf,df->td', grad_gate, w_gate, preferred_ele...  83.6 us
    all_gather x1, waiting for transfers between devices, per_device(): lax.all_gather(tokens, 'mp', axis=1, tiled=True)  80.2 us
    psum x1, waiting for transfers between devices, per_device(): hid_gate, hid_up, hid_down = lax.psum((hid_gate, hid_up, hid_down), 'mp')  65.8 us
    all_gather x1, waiting for transfers between devices, per_device(): lax.all_gather(cotangent, 'mp', axis=1, tiled=True)  43.5 us
    gather x1, local copies, waits for them, and re-layouts, per_device(): jnp.take(lax.all_gather(cotangent, 'mp', axis=1, tiled=True), positions,...  13.2 us
    gather x1, local copies, waits for them, and re-layouts, per_device(): jnp.take(lax.all_gather(tokens, 'mp', axis=1, tiled=True), positions, axi...  13 us
    dot_general x1, matrix products, per_device(): jnp.einsum('tf,df->td', grad_up, w_up, preferred_element_type=jnp.float32)  11.3 us
    dot_general x1, matrix products, per_device(): jnp.dot(span_x, w_up, preferred_element_type=jnp.float32)  11 us
  transfers between devices with their start and end apart: 4, of which 4 were waited for; matrix products, arithmetic and copies ran while one was open for 15% of the time, Pallas kernels for 0%

commit v1 on v0

v1 whole, which is shorter than its diff:
```python
import jax
import jax.numpy as jnp
from jax import lax
from jax.experimental import pallas as pl
from jax.experimental.pallas import tpu as pltpu
from jax.sharding import PartitionSpec as P

RANK = 64
SPAN_LEN = 64
SPANS = 8
ROWS = SPANS * SPAN_LEN
PIECE = 256
FTILE = 128
NF = 7
FSHARD = NF * FTILE
HALF = 2048
PROJ = 256
BF = jnp.bfloat16
F32 = jnp.float32
NT = (((1,), (1,)), ((), ()))
TN = (((0,), (0,)), ((), ()))


def shift(v, dx, dy):
    pairs = [(4 * x + y, 4 * ((x + dx) % 4) + (y + dy) % 4) for x in range(4) for y in range(4)]
    return lax.ppermute(v, "mp", pairs)


def whole(shape):
    return pl.BlockSpec(shape, lambda *_: (0,) * len(shape))


def gather_kernel(off, tok, cot, xo, go):
    col = lax.broadcasted_iota(jnp.int32, (SPAN_LEN, 128), 1)
    row = lax.broadcasted_iota(jnp.int32, (SPAN_LEN, 128), 0)
    for s in range(SPANS):
        o = off[s]
        start = pl.multiple_of(jnp.minimum((o // 16) * 16, 1024 - 128), 16)
        pick = jnp.where(col == row + (o - start), 1.0, 0.0).astype(BF)
        out = slice(s * SPAN_LEN, (s + 1) * SPAN_LEN)
        xo[out, :] = jnp.dot(pick, tok[pl.ds(start, 128), :], preferred_element_type=F32).astype(BF)
        go[out, :] = jnp.dot(pick, cot[pl.ds(start, 128), :], preferred_element_type=F32).astype(BF)


def gather(offsets, tokens, cotangent):
    o = jax.ShapeDtypeStruct((ROWS, PIECE), BF)
    return pl.pallas_call(
        gather_kernel,
        in_specs=[pl.BlockSpec(memory_space=pltpu.SMEM), pl.BlockSpec(memory_space=pltpu.VMEM),
                  pl.BlockSpec(memory_space=pltpu.VMEM)],
        out_shape=(o, o),
        cost_estimate=pl.CostEstimate(flops=10**8, bytes_accessed=2 * 10**6, transcendentals=0),
        name="span_rows",
    )(offsets, tokens, cotangent)


def stage(me, xp, gp, wg, wu, wd, fpt, acc, hpt=None):
    first, last = acc is None, hpt is not None

    def body(me_ref, *refs):
        refs = list(refs)
        take = lambda n: [refs.pop(0) for _ in range(n)]
        xs, gs, wgs, wus, wds, fxs, fgs = (take(4) for _ in range(7))
        if not first:
            acc_in, feat_in = take(2)
        if last:
            hp, gg_o, gu_o, proj_o, hid, feat = take(6)
        else:
            acc_o, feat = take(2)
        n = pl.program_id(0)
        @pl.when(n == 0)
        def _():
            fx = lax.dot_general(jnp.concatenate([r[...] for r in xs], axis=1), jnp.concatenate([r[...] for r in fxs], axis=1), NT, preferred_element_type=F32)
            fg = lax.dot_general(jnp.concatenate([r[...] for r in gs], axis=1), jnp.concatenate([r[...] for r in fgs], axis=1), NT, preferred_element_type=F32)
            if first:
                feat[:, :128] = fx
                feat[:, 128:192] = fg
            else:
                feat[:, :128] = fx + feat_in[:, :128]
                feat[:, 128:192] = fg + feat_in[:, 128:192]
            if last:
                hid[...] = jnp.zeros_like(hid)

        x = jnp.concatenate([r[...] for r in xs], axis=1)
        g = jnp.concatenate([r[...] for r in gs], axis=1)
        rhs = jnp.concatenate(
            [jnp.concatenate([r[...] for r in wgs], axis=0), jnp.concatenate([r[...] for r in wus], axis=0)], axis=1)
        gate_up = jnp.dot(x, rhs, preferred_element_type=F32)
        down = lax.dot_general(g, jnp.concatenate([r[...] for r in wds], axis=1), NT, preferred_element_type=F32)
        if not first:
            gate_up += acc_in[0, :, :256]
            down += acc_in[0, :, 256:]

        if not last:
            acc_o[0, :, :256] = gate_up
            acc_o[0, :, 256:] = down
            return
        gate, up = gate_up[:, :128], gate_up[:, 128:]
        sig = jax.nn.sigmoid(gate)
        act = gate * sig
        hidden = (act * up).astype(BF)
        grad_gate = (down * up * sig * (1.0 + gate * (1.0 - sig))).astype(BF)
        grad_up = (down * act).astype(BF)
        gg_o[...] = grad_gate
        gu_o[...] = grad_up
        for k, v in enumerate((grad_gate, grad_up, hidden)):
            sl = slice(k * RANK, (k + 1) * RANK)
            hid[:, sl] += lax.dot_general(v, hp[sl, :], NT, preferred_element_type=F32)

        @pl.when(n == NF - 1)
        def _():
            for q in range(4):
                halves = []
                for s in (2 * q, 2 * q + 1):
                    r = slice(s * SPAN_LEN, (s + 1) * SPAN_LEN)
                    left = jnp.concatenate([feat[r, :128], hid[r, 128:192]], axis=1)
                    right = jnp.concatenate([hid[r, :128], feat[r, 128:192]], axis=1)
                    halves.append(lax.dot_general(left, right, TN, precision=lax.Precision.HIGHEST,
                                                  preferred_element_type=F32))
                for k in range(3):
                    d = slice(k * RANK, (k + 1) * RANK)
                    proj_o[q, d, :] = jnp.concatenate([halves[0][d, d], halves[1][d, d]], axis=1).astype(BF)

    def block(d):
        dx, dy = d
        return lambda m: 4 * ((m[0] // 4 + dx) % 4) + (m[0] % 4 + dy) % 4

    def piece(part):
        return pl.BlockSpec((ROWS, PIECE), lambda n, m: (part, 0))

    specs, ops = [], []
    for group in (xp, gp):
        for arr, part, _ in group:
            specs.append(piece(part))
            ops.append(arr)
    bx = [block(d) for _, _, d in xp]
    bg = [block(d) for _, _, d in gp]
    for w in (wg, wu):
        for b in bx:
            specs.append(pl.BlockSpec((PIECE, FTILE), lambda n, m, b=b: (b(m), n)))
            ops.append(w)
    for b in bg:
        specs.append(pl.BlockSpec((FTILE, PIECE), lambda n, m, b=b: (n, b(m))))
        ops.append(wd)
    for b in bx:
        specs.append(pl.BlockSpec((128, PIECE), lambda n, m, b=b: (0, b(m))))
        ops.append(fpt)
    for b in bg:
        specs.append(pl.BlockSpec((RANK, PIECE), lambda n, m, b=b: (2, b(m))))
        ops.append(fpt)
    acc_spec = pl.BlockSpec((1, ROWS, 384), lambda n, m: (n, 0, 0))
    feat_spec = whole((ROWS, 192))
    acc_shape = jax.ShapeDtypeStruct((NF, ROWS, 384), F32)
    feat_shape = jax.ShapeDtypeStruct((ROWS, 192), F32)
    if not first:
        specs += [acc_spec, feat_spec]
        ops += list(acc)
    scratch = []
    if last:
        specs.append(pl.BlockSpec((192, FTILE), lambda n, m: (0, n)))
        ops.append(hpt)
        tile = pl.BlockSpec((ROWS, FTILE), lambda n, m: (0, n))
        out_specs = [tile, tile, whole((4, 192, 128))]
        out_shape = [jax.ShapeDtypeStruct((ROWS, FSHARD), BF)] * 2 + [jax.ShapeDtypeStruct((4, 192, 128), BF)]
        scratch = [pltpu.VMEM((ROWS, 192), F32), pltpu.VMEM((ROWS, 192), F32)]
    else:
        out_specs = [acc_spec, feat_spec]
        out_shape = [acc_shape, feat_shape]
    return pl.pallas_call(
        body,
        grid_spec=pltpu.PrefetchScalarGridSpec(num_scalar_prefetch=1, grid=(NF,), in_specs=specs,
                                               out_specs=out_specs, scratch_shapes=scratch),
        out_shape=out_shape,
        cost_estimate=pl.CostEstimate(flops=3 * 2 * ROWS * 1024 * FSHARD, bytes_accessed=20 * 10**6, transcendentals=0),
        name="forward_last" if last else ("forward_first" if first else "forward_mid"),
    )(me, *ops)


ORDER = (0, 1, 3, 2)


def input_grad(me, gg, gu, wg, wu, base, by_x, proj=None):
    width = HALF + (PROJ if proj is not None else 0)

    def body(me_ref, *refs):
        refs = list(refs)
        gg_r, gu_r, wg_r, wu_r = refs[:4]
        outs, rows = refs[-5:-1], refs[-1]
        n = pl.program_id(0)

        @pl.when(n == 0)
        def _():
            x, y = me_ref[0] // 4, me_ref[0] % 4
            for j, d in enumerate(ORDER):
                if by_x:
                    src = [pl.multiple_of(((x + d) % 4) * 128, 128)]
                    size = 128
                else:
                    src = [pl.multiple_of(128 * b + ((y + d) % 4) * 32, 32) for b in range(4)]
                    size = 32
                for b, at in enumerate(src):
                    dst = slice(j * 128 + b * size, j * 128 + (b + 1) * size)
                    rows[dst, :FSHARD] = gg_r[pl.ds(at, size), :]
                    rows[dst, FSHARD:] = gu_r[pl.ds(at, size), :]
                if proj is not None:
                    block = refs[4][(x + d) % 4]
                    outs[j][:, HALF : HALF + 128] = block[:128]
                    outs[j][:64, HALF + 128 :] = block[128:]
                    outs[j][64:, HALF + 128 :] = jnp.zeros((64, 128), BF)

        rhs = jnp.concatenate([wg_r[...], wu_r[...]], axis=1)
        res = lax.dot_general(rows[...], rhs, NT, preferred_element_type=F32).astype(BF)
        for t in range(2):

            @pl.when(n == t)
            def _():
                for j in range(4):
                    outs[j][:, t * 1024 : (t + 1) * 1024] = res[j * 128 : (j + 1) * 128]

    w_spec = pl.BlockSpec((1024, FSHARD), lambda n, m: (base + n, 0))
    specs = [whole((ROWS, FSHARD)), whole((ROWS, FSHARD)), w_spec, w_spec]
    ops = [gg, gu, wg, wu]
    if proj is not None:
        specs.append(whole((4, 192, 128)))
        ops.append(proj)
    return pl.pallas_call(
        body,
        grid_spec=pltpu.PrefetchScalarGridSpec(
            num_scalar_prefetch=1, grid=(2,), in_specs=specs, out_specs=[whole((128, width))] * 4,
            scratch_shapes=[pltpu.VMEM((ROWS, 2 * FSHARD), BF)]),
        out_shape=[jax.ShapeDtypeStruct((128, width), BF)] * 4,
        cost_estimate=pl.CostEstimate(flops=2 * ROWS * 2 * FSHARD * HALF, bytes_accessed=12 * 10**6, transcendentals=0),
        name="input_grad_x" if by_x else "input_grad_y",
    )(me, *ops)


def middle_sum(me, blocks, with_proj):
    width = blocks[0].shape[1]
    out_width = HALF + (6 * 128 if with_proj else 0)

    def body(me_ref, b0, b1, b2, b3, o0, o1, o2, o3, total):
        mine = me_ref[0] % 4 if with_proj else me_ref[0] // 4
        total[...] = (b0[...].astype(F32) + b1[...].astype(F32) + b2[...].astype(F32) + b3[...].astype(F32))
        for j, (d, o) in enumerate(zip(ORDER, (o0, o1, o2, o3))):
            at = pl.multiple_of(((mine + d) % 4) * 32, 32)
            o[:, :HALF] = total[pl.ds(at, 32), :HALF].astype(BF)
            if with_proj:
                for k in range(6):
                    lane = HALF + 128 * (k // 4)
                    o[:, HALF + k * 128 : HALF + (k + 1) * 128] = total[(k % 4) * 32 : (k % 4 + 1) * 32,
                                                                       lane : lane + 128].astype(BF)

    v = pl.BlockSpec(memory_space=pltpu.VMEM)
    return pl.pallas_call(
        body,
        in_specs=[pl.BlockSpec(memory_space=pltpu.SMEM)] + [v] * 4,
        out_specs=[v] * 4,
        out_shape=[jax.ShapeDtypeStruct((32, out_width), BF)] * 4,
        scratch_shapes=[pltpu.VMEM((128, width), F32)],
        cost_estimate=pl.CostEstimate(flops=10**6, bytes_accessed=3 * 10**6, transcendentals=0),
        name="middle_sum_x" if with_proj else "middle_sum_y",
    )(me, *blocks)


def final_sum_x(me, blocks):
    def body(me_ref, b0, b1, b2, b3, o, p, slots):
        y = me_ref[0] % 4
        o[...] = (b0[:, :HALF].astype(F32) + b1[:, :HALF].astype(F32) + b2[:, :HALF].astype(F32)
                  + b3[:, :HALF].astype(F32)).astype(BF)
        for d, b in zip(ORDER, (b0, b1, b2, b3)):
            slots[(y + 4 - d) % 4] = b[:, HALF:].astype(F32)
        total = ((slots[0] + slots[1]) + (slots[2] + slots[3])).astype(BF)
        for k in range(6):
            p[k * 32 : (k + 1) * 32, :] = total[:, k * 128 : (k + 1) * 128]

    v = pl.BlockSpec(memory_space=pltpu.VMEM)
    return pl.pallas_call(
        body,
        in_specs=[pl.BlockSpec(memory_space=pltpu.SMEM)] + [v] * 4,
        out_specs=[v] * 2,
        out_shape=[jax.ShapeDtypeStruct((32, HALF), BF), jax.ShapeDtypeStruct((192, 128), BF)],
        scratch_shapes=[pltpu.VMEM((4, 32, 6 * 128), F32)],
        cost_estimate=pl.CostEstimate(flops=10**6, bytes_accessed=10**6, transcendentals=0),
        name="final_sum_x",
    )(me, *blocks)


def final_sum_y(left, blocks):
    def body(l, b0, b1, b2, b3, o):
        o[:, :HALF] = l[...]
        o[:, HALF:] = (b0[...].astype(F32) + b1[...].astype(F32) + b2[...].astype(F32) + b3[...].astype(F32)).astype(BF)

    v = pl.BlockSpec(memory_space=pltpu.VMEM)
    return pl.pallas_call(
        body, in_specs=[v] * 5, out_specs=v, out_shape=jax.ShapeDtypeStruct((32, 2 * HALF), BF),
        cost_estimate=pl.CostEstimate(flops=10**6, bytes_accessed=10**6, transcendentals=0),
        name="final_sum_y",
    )(left, *blocks)


def assemble(me, blocks):
    def body(me_ref, b0, b1, b2, b3, o):
        x = me_ref[0] // 4
        for d, b in zip(ORDER, (b0, b1, b2, b3)):
            src = (x + 4 - d) % 4
            for k in range(3):
                for h in range(2):
                    o[k, 2 * src + h] = b[k * 64 : (k + 1) * 64, h * 64 : (h + 1) * 64].astype(F32)

    v = pl.BlockSpec(memory_space=pltpu.VMEM)
    return pl.pallas_call(
        body, in_specs=[pl.BlockSpec(memory_space=pltpu.SMEM)] + [v] * 4, out_specs=v,
        out_shape=jax.ShapeDtypeStruct((3, SPANS, RANK, RANK), F32),
        cost_estimate=pl.CostEstimate(flops=10**6, bytes_accessed=10**6, transcendentals=0),
        name="assemble",
    )(me, *blocks)


def per_device(tokens, cotangent, offsets, w_gate, w_up, w_down, feature_proj, hidden_proj):
    me = lax.axis_index("mp").astype(jnp.int32).reshape(1)
    fpt, hpt = feature_proj.T, hidden_proj.T
    xs, gs = gather(offsets, tokens, cotangent)

    sx = lambda v, d: shift(v, 0, d)
    sy = lambda v, d: shift(v, d, 0)

    def first_axis(own, sh):
        return [own, sh(own, 1), sh(own, -1), sh(own, 2)]

    x1 = first_axis(xs, sx)
    g1 = first_axis(gs, sy)
    pos1 = (0, -1, 1, 2)

    def second_axis(p, sh):
        a = jnp.concatenate([p[0], p[1]], axis=0)
        b = jnp.concatenate([p[2], p[3]], axis=0)
        a_lo, a_hi = sh(a, 1), sh(a, -1)
        b_lo, b_hi = sh(b, 1), sh(b, -1)
        a_far, b_far = sh(a_lo, 1), sh(b_hi, -1)
        return a_lo, a_hi, b_lo, b_hi, a_far, b_far

    xa_lo, xa_hi, xb_lo, xb_hi, xa_far, xb_far = second_axis(x1, sy)
    ga_lo, ga_hi, gb_lo, gb_hi, ga_far, gb_far = second_axis(g1, sx)

    def xpair(arr, which, d):
        return [(arr, i, (d, pos1[2 * which + i])) for i in range(2)]

    def gpair(arr, which, d):
        return [(arr, i, (pos1[2 * which + i], d)) for i in range(2)]

    w = (w_gate, w_up, w_down, fpt)
    acc = stage(me, [(x1[i], 0, (0, pos1[i])) for i in range(4)], [(g1[i], 0, (pos1[i], 0)) for i in range(4)], *w, None)
    acc = stage(me, xpair(xa_lo, 0, -1) + xpair(xa_hi, 0, 1), gpair(ga_lo, 0, -1) + gpair(ga_hi, 0, 1), *w, acc)
    acc = stage(me, xpair(xb_lo, 1, -1) + xpair(xb_hi, 1, 1), gpair(gb_lo, 1, -1) + gpair(gb_hi, 1, 1), *w, acc)
    grad_gate, grad_up, proj = stage(me, xpair(xa_far, 0, 2) + xpair(xb_far, 1, 2),
                                     gpair(ga_far, 0, 2) + gpair(gb_far, 1, 2), *w, acc, hpt)

    bx = input_grad(me, grad_gate, grad_up, w_gate, w_up, 0, True, proj)
    rx = [bx[0]] + [sy(bx[j], d) for j, d in ((1, 1), (2, -1), (3, 2))]
    by = input_grad(me, grad_gate, grad_up, w_gate, w_up, 2, False)
    ry = [by[0]] + [sx(by[j], d) for j, d in ((1, 1), (2, -1), (3, 2))]
    mx = middle_sum(me, rx, True)
    qx = [mx[0]] + [sx(mx[j], d) for j, d in ((1, 1), (2, -1), (3, 2))]
    my = middle_sum(me, ry, False)
    qy = [my[0]] + [sy(my[j], d) for j, d in ((1, 1), (2, -1), (3, 2))]
    left, p = final_sum_x(me, qx)
    ps = [p] + [sy(p, d) for d in (1, -1, 2)]
    return final_sum_y(left, qy), assemble(me, ps)


def solution(mesh):
    in_specs = (
        P("dp", "mp"),
        P("dp", "mp"),
        P("dp"),
        P(None, "mp"),
        P(None, "mp"),
        P("mp", None),
        P(),
        P("mp", None),
    )
    out_specs = (P(("dp", "mp"), None), P(None, "dp", None, None))
    return jax.shard_map(
        per_device, mesh=mesh, in_specs=in_specs, out_specs=out_specs, check_vma=False
    )
```

time: 388 us -> 173 us (0.45)
  waiting for transfers between devices: 274 us -> 24.6 us
  Pallas kernels: 0 us -> 82.8 us
  matrix products: 65.4 us -> 0 us
  starting transfers between devices: 0.16 us -> 50.6 us
  local copies, waits for them, and re-layouts: 30.1 us -> 12.9 us
  between operations: 13.9 us -> 0.89 us
    all_gather x2 -> x0, waiting for transfers between devices: 124 us -> none  [the longest x1 80.2 us: per_device(): lax.all_gather(tokens, 'mp', axis=1, tiled=True)]
    reduce_scatter x1 -> x0, waiting for transfers between devices: 83.6 us -> none  [per_device(): lax.psum_scatter(jnp.einsum('tf,df->td', grad_gate, w_gate, preferred_ele...]
    pallas_call x0 -> x12, Pallas kernels: none -> 82.8 us  [the longest x4 51.9 us: stage(): pl.pallas_call(body, grid_spec=pltpu.PrefetchScalarGridSpec(num_scalar_pr...]
    psum x1 -> x0, waiting for transfers between devices: 65.8 us -> none  [per_device(): hid_gate, hid_up, hid_down = lax.psum((hid_gate, hid_up, hid_down), 'mp')]
    dot_general x10 -> x0, matrix products: 59.7 us -> none  [the longest x1 11.3 us: per_device(): jnp.einsum('tf,df->td', grad_up, w_up, preferred_element_type=jnp.float32)]
    ppermute x0 -> x33, starting transfers between devices: none -> 50.6 us  [shift(): return lax.ppermute(v, 'mp', pairs)]
    gather x2 -> x0, local copies, waits for them, and re-layouts: 26.3 us -> none  [the longest x1 13.2 us: per_device(): jnp.take(lax.all_gather(cotangent, 'mp', axis=1, tiled=True), positions,...]
    ppermute x0 -> x33, waiting for transfers between devices: none -> 24.6 us  [shift(): return lax.ppermute(v, 'mp', pairs)]
  transfers between devices with their start and end apart: 4 -> 33, of which waited for: 4 -> 10; matrix products, arithmetic and copies ran while one was open for 15% -> 4% of each run, Pallas kernels for 0% -> 32%
where the time goes in v1:
time: 173 us; the launch traced here: 172 us
  Pallas kernels  82.8 us (48%)
  starting transfers between devices  50.6 us (29%)
  waiting for transfers between devices  24.6 us (14%)
  local copies, waits for them, and re-layouts  12.9 us (7%)
    pallas_call x4, Pallas kernels, stage(): pl.pallas_call(body, grid_spec=pltpu.PrefetchScalarGridSpec(num_scalar_pr...  51.9 us
    ppermute x33, starting transfers between devices, shift(): return lax.ppermute(v, 'mp', pairs)  50.6 us
    ppermute x33, waiting for transfers between devices, shift(): return lax.ppermute(v, 'mp', pairs)  24.6 us
    pallas_call x2, Pallas kernels, input_grad(): pl.pallas_call(body, grid_spec=pltpu.PrefetchScalarGridSpec(num_scalar_pr...  17.1 us
    unnamed x60, local copies, waits for them, and re-layouts  9.97 us
    pallas_call x2, Pallas kernels, middle_sum(): pl.pallas_call(body, in_specs=[pl.BlockSpec(memory_space=pltpu.SMEM)] + [...  5.73 us
  transfers between devices with their start and end apart: 33, of which 10 were waited for; matrix products, arithmetic and copies ran while one was open for 4% of the time, Pallas kernels for 32%

profile of v1, /device:TPU:0, one launch (start us, length us, event | category | flops | bytes accessed | tf_op | source)
XLA Modules:
  0.0 171.8 jit_solution(931318669404861291)
XLA Ops:
  0.6 2.3 %span_rows.1 = (bf16[512,256]{1,0:T(8,128)(2,1)}, bf16[512,256]{1,0:T(8,128)(2,1)}) custom-call(s32[8]{0:T(128)} %off.1, bf16[1024,256]{1,0:T(8,128)(2,1)} %tok.1, bf16[1024,256]{1,0:T(8,128)(2,1)} %cot.1), custom_call_target="tpu_custom_call" | custom-call | flops 100000000 | bytes 2000000 | tf_op jit(solution)/shard_map/span_rows/pallas_call | solution.py:47
  18.5 2.2 %collective-permute-start.3 = (bf16[512,256]{1,0:T(8,128)(2,1)}, bf16[512,256]{1,0:T(8,128)(2,1)S(1)}, u32[]{:S(2)}, u32[]{:S(2)}) collective-permute-start(bf16[512,256]{1,0:T(8,128)(2,1)} %get-tuple-element.31.refs_0_), channel_id=1, source_target_pairs={{0,3},{1,0},{2,1},{3,2},{4,7},{5,4},{6,5},{7,6},{8,11},{9,8},{10,9... | collective-permute-start | bytes 786440 | tf_op jit(solution)/shard_map/ppermute | solution.py:26
  21.5 2.4 %collective-permute-start.17 = (bf16[1024,256]{1,0:T(8,128)(2,1)}, bf16[1024,256]{1,0:T(8,128)(2,1)S(1)}, u32[]{:S(2)}, u32[]{:S(2)}) collective-permute-start(bf16[1024,256]{1,0:T(8,128)(2,1)} %constant_dynamic-update-slice_fusion.4), channel_id=1, source_target_pairs={{0,3},{1,0},{2,1},{3,2},{4,7},{5,4},{6,5},{7,6},{8,11},{9,8},{10,9... | collective-permute-start | bytes 1572872 | tf_op jit(solution)/shard_map/ppermute | solution.py:26
  24.6 7.2 %collective-permute-done.3.refs_2_ = bf16[512,256]{1,0:T(8,128)(2,1)S(1)} collective-permute-done((bf16[512,256]{1,0:T(8,128)(2,1)}, bf16[512,256]{1,0:T(8,128)(2,1)S(1)}, u32[]{:S(2)}, u32[]{:S(2)}) %collective-permute-start.3) | collective-permute-done | bytes 262176 | tf_op jit(solution)/shard_map/ppermute | solution.py:26
  31.7 4.1 %collective-permute-start.12 = (bf16[1024,256]{1,0:T(8,128)(2,1)}, bf16[1024,256]{1,0:T(8,128)(2,1)S(1)}, u32[]{:S(2)}, u32[]{:S(2)}) collective-permute-start(bf16[1024,256]{1,0:T(8,128)(2,1)} %constant_dynamic-update-slice_fusion.6), channel_id=1, source_target_pairs={{0,3},{1,0},{2,1},{3,2},{4,7},{5,4},{6,5},{7,6},{8,11},{9,8},{10,9... | collective-permute-start | bytes 1572872 | tf_op jit(solution)/shard_map/ppermute | solution.py:26
  38.0 2.3 %collective-permute-start.5 = (bf16[1024,256]{1,0:T(8,128)(2,1)}, bf16[1024,256]{1,0:T(8,128)(2,1)S(1)}, u32[]{:S(2)}, u32[]{:S(2)}) collective-permute-start(bf16[1024,256]{1,0:T(8,128)(2,1)} %constant_dynamic-update-slice_fusion.2), channel_id=1, source_target_pairs={{0,12},{1,13},{2,14},{3,15},{4,0},{5,1},{6,2},{7,3},{8,4},{9,5},{1... | collective-permute-start | bytes 1572872 | tf_op jit(solution)/shard_map/ppermute | solution.py:26
  40.4 2.0 %collective-permute-start.14 = (bf16[1024,256]{1,0:T(8,128)(2,1)}, bf16[1024,256]{1,0:T(8,128)(2,1)S(1)}, u32[]{:S(2)}, u32[]{:S(2)}) collective-permute-start(bf16[1024,256]{1,0:T(8,128)(2,1)} %constant_dynamic-update-slice_fusion.2), channel_id=1, source_target_pairs={{0,4},{1,5},{2,6},{3,7},{4,8},{5,9},{6,10},{7,11},{8,12},{9,13},{1... | collective-permute-start | bytes 1572872 | tf_op jit(solution)/shard_map/ppermute | solution.py:26
  42.4 2.3 %collective-permute-done.17.refs_6_.refs_7_ = bf16[1024,256]{1,0:T(8,128)(2,1)S(1)} collective-permute-done((bf16[1024,256]{1,0:T(8,128)(2,1)}, bf16[1024,256]{1,0:T(8,128)(2,1)S(1)}, u32[]{:S(2)}, u32[]{:S(2)}) %collective-permute-start.17) | collective-permute-done | bytes 524320 | tf_op jit(solution)/shard_map/ppermute | solution.py:26
  44.9 11.7 %forward_first.1 = (f32[7,512,384]{2,1,0:T(8,128)}, f32[512,192]{1,0:T(8,128)}) custom-call(s32[1]{0:T(128)} %bitcast.me_ref, bf16[512,256]{1,0:T(8,128)(2,1)} %get-tuple-element.31.refs_0_, bf16[512,256]{1,0:T(8,128)(2,1)} %copy-done.10, bf16[512,256]{1,0:T(8,128)(2,1)} %copy-done.11, bf16[512,256]{1,0:T(8,128)(2,1)} %copy-done.12, ...), custom_call_target="tpu_custom_call" | custom-call | flops 2818572288 | bytes 20000000 | tf_op jit(solution)/shard_map/forward_first/pallas_call | solution.py:169
  56.6 3.1 %collective-permute-start.13 = (bf16[1024,256]{1,0:T(8,128)(2,1)S(1)}, bf16[1024,256]{1,0:T(8,128)(2,1)S(1)}, u32[]{:S(2)}, u32[]{:S(2)}) collective-permute-start(bf16[1024,256]{1,0:T(8,128)(2,1)S(1)} %collective-permute-done.12.refs_6_.refs_7_), channel_id=1, source_target_pairs={{0,3},{1,0},{2,1},{3,2},{4,7},{5,4},{6,5},{7,6},{8,11},{9,8},{10,9... | collective-permute-start | bytes 1572872 | tf_op jit(solution)/shard_map/ppermute | solution.py:26
  59.7 2.6 %collective-permute-start.6 = (bf16[1024,256]{1,0:T(8,128)(2,1)S(1)}, bf16[1024,256]{1,0:T(8,128)(2,1)}, u32[]{:S(2)}, u32[]{:S(2)}) collective-permute-start(bf16[1024,256]{1,0:T(8,128)(2,1)S(1)} %collective-permute-done.5.refs_2_.refs_3_), channel_id=1, source_target_pairs={{0,12},{1,13},{2,14},{3,15},{4,0},{5,1},{6,2},{7,3},{8,4},{9,5},{1... | collective-permute-start | bytes 1572872 | tf_op jit(solution)/shard_map/ppermute | solution.py:26
  64.6 12.5 %forward_mid.2 = (f32[7,512,384]{2,1,0:T(8,128)}, f32[512,192]{1,0:T(8,128)}) custom-call(s32[1]{0:T(128)} %bitcast.me_ref, bf16[1024,256]{1,0:T(8,128)(2,1)} %copy-done.1, bf16[1024,256]{1,0:T(8,128)(2,1)} %copy-done.1, bf16[1024,256]{1,0:T(8,128)(2,1)} %collective-permute-done.16.refs_2_.refs_3_, ...), custom_call_target="tpu_custom_call" | custom-call | flops 2818572288 | bytes 20000000 | tf_op jit(solution)/shard_map/forward_mid/pallas_call | solution.py:169
  77.1 12.5 %forward_mid.3 = (f32[7,512,384]{2,1,0:T(8,128)}, f32[512,192]{1,0:T(8,128)}) custom-call(s32[1]{0:T(128)} %bitcast.me_ref, bf16[1024,256]{1,0:T(8,128)(2,1)} %copy-done.5, bf16[1024,256]{1,0:T(8,128)(2,1)} %copy-done.5, bf16[1024,256]{1,0:T(8,128)(2,1)} %copy-done.3, bf16[1024,256]{1,0:T(8,128)(2,1)} %copy-done.3, ...), custom_call_target="tpu_custom_call" | custom-call | flops 2818572288 | bytes 20000000 | tf_op jit(solution)/shard_map/forward_mid/pallas_call | solution.py:169
  90.4 15.3 %forward_last.1 = (bf16[512,896]{1,0:T(8,128)(2,1)}, bf16[512,896]{1,0:T(8,128)(2,1)}, bf16[4,192,128]{2,1,0:T(8,128)(2,1)}) custom-call(s32[1]{0:T(128)} %bitcast.me_ref, bf16[1024,256]{1,0:T(8,128)(2,1)} %collective-permute-done.2.refs_0_.refs_1_, bf16[1024,256]{1,0:T(8,128)(2,1)} %collective-permute-done.2.refs_0_.refs_1_, ...), custom_call_target="tpu_custom_call" | custom-call | flops 2818572288 | bytes 20000000 | tf_op jit(solution)/shard_map/forward_last/pallas_call | solution.py:169
  105.7 8.6 %input_grad_x.1 = (bf16[128,2304]{1,0:T(8,128)(2,1)}, bf16[128,2304]{1,0:T(8,128)(2,1)}, bf16[128,2304]{1,0:T(8,128)(2,1)}, bf16[128,2304]{1,0:T(8,128)(2,1)}) custom-call(s32[1]{0:T(128)} %bitcast.me_ref, bf16[512,896]{1,0:T(8,128)(2,1)} %get-tuple-element.39.refs_0_, bf16[512,896]{1,0:T(8,128)(2,1)} %get-tuple-element.40.refs_1_, ...), custom_call_target="tpu_custom_call" | custom-call | flops 3758096384 | bytes 12000000 | tf_op jit(solution)/shard_map/input_grad_x/pallas_call | solution.py:226
  114.4 3.2 %collective-permute-start.19 = (bf16[128,2304]{1,0:T(8,128)(2,1)}, bf16[128,2304]{1,0:T(8,128)(2,1)S(1)}, u32[]{:S(2)}, u32[]{:S(2)}) collective-permute-start(bf16[128,2304]{1,0:T(8,128)(2,1)} %get-tuple-element.44), channel_id=1, source_target_pairs={{0,12},{1,13},{2,14},{3,15},{4,0},{5,1},{6,2},{7,3},{8,4},{9,5},{1... | collective-permute-start | bytes 1769480 | tf_op jit(solution)/shard_map/ppermute | solution.py:26
  119.0 8.4 %input_grad_y.1 = (bf16[128,2048]{1,0:T(8,128)(2,1)}, bf16[128,2048]{1,0:T(8,128)(2,1)}, bf16[128,2048]{1,0:T(8,128)(2,1)}, bf16[128,2048]{1,0:T(8,128)(2,1)}) custom-call(s32[1]{0:T(128)} %bitcast.me_ref, bf16[512,896]{1,0:T(8,128)(2,1)} %get-tuple-element.39.refs_0_, bf16[512,896]{1,0:T(8,128)(2,1)} %get-tuple-element.40.refs_1_, ...), custom_call_target="tpu_custom_call" | custom-call | flops 3758096384 | bytes 12000000 | tf_op jit(solution)/shard_map/input_grad_y/pallas_call | solution.py:226
  127.4 3.2 %collective-permute-start.25 = (bf16[128,2048]{1,0:T(8,128)(2,1)}, bf16[128,2048]{1,0:T(8,128)(2,1)S(1)}, u32[]{:S(2)}, u32[]{:S(2)}) collective-permute-start(bf16[128,2048]{1,0:T(8,128)(2,1)} %get-tuple-element.53), channel_id=1, source_target_pairs={{0,3},{1,0},{2,1},{3,2},{4,7},{5,4},{6,5},{7,6},{8,11},{9,8},{10,9... | collective-permute-start | bytes 1572872 | tf_op jit(solution)/shard_map/ppermute | solution.py:26
  132.5 2.2 %collective-permute-done.19.b2 = bf16[128,2304]{1,0:T(8,128)(2,1)S(1)} collective-permute-done((bf16[128,2304]{1,0:T(8,128)(2,1)}, bf16[128,2304]{1,0:T(8,128)(2,1)S(1)}, u32[]{:S(2)}, u32[]{:S(2)}) %collective-permute-start.19) | collective-permute-done | bytes 589856 | tf_op jit(solution)/shard_map/ppermute | solution.py:26
  137.3 3.0 %middle_sum_x.1 = (bf16[32,2816]{1,0:T(8,128)(2,1)}, bf16[32,2816]{1,0:T(8,128)(2,1)}, bf16[32,2816]{1,0:T(8,128)(2,1)}, bf16[32,2816]{1,0:T(8,128)(2,1)}) custom-call(s32[1]{0:T(128)} %bitcast.me_ref, bf16[128,2304]{1,0:T(8,128)(2,1)} %get-tuple-element.42.b0, bf16[128,2304]{1,0:T(8,128)(2,1)} %copy-done.13, bf16[128,2304]{1,0:T(8,128)(2,1)} %copy-done.14, ...), custom_call_target="tpu_custom_call" | custom-call | flops 1000000 | bytes 3000000 | tf_op jit(solution)/shard_map/middle_sum_x/pallas_call | solution.py:254
  144.7 3.7 %collective-permute-done.25.b2 = bf16[128,2048]{1,0:T(8,128)(2,1)S(1)} collective-permute-done((bf16[128,2048]{1,0:T(8,128)(2,1)}, bf16[128,2048]{1,0:T(8,128)(2,1)S(1)}, u32[]{:S(2)}, u32[]{:S(2)}) %collective-permute-start.25) | collective-permute-done | bytes 524320 | tf_op jit(solution)/shard_map/ppermute | solution.py:26
  150.6 2.8 %middle_sum_y.1 = (bf16[32,2048]{1,0:T(8,128)(2,1)}, bf16[32,2048]{1,0:T(8,128)(2,1)}, bf16[32,2048]{1,0:T(8,128)(2,1)}, bf16[32,2048]{1,0:T(8,128)(2,1)}) custom-call(s32[1]{0:T(128)} %bitcast.me_ref, bf16[128,2048]{1,0:T(8,128)(2,1)} %get-tuple-element.51.b0, bf16[128,2048]{1,0:T(8,128)(2,1)} %copy-done.16, bf16[128,2048]{1,0:T(8,128)(2,1)} %copy-done.17, ...), custom_call_target="tpu_custom_call" | custom-call | flops 1000000 | bytes 3000000 | tf_op jit(solution)/shard_map/middle_sum_y/pallas_call | solution.py:254
  154.5 2.1 %collective-permute-start.28 = (bf16[32,2048]{1,0:T(8,128)(2,1)}, bf16[32,2048]{1,0:T(8,128)(2,1)S(1)}, u32[]{:S(2)}, u32[]{:S(2)}) collective-permute-start(bf16[32,2048]{1,0:T(8,128)(2,1)} %get-tuple-element.57), channel_id=1, source_target_pairs={{0,12},{1,13},{2,14},{3,15},{4,0},{5,1},{6,2},{7,3},{8,4},{9,5},{1... | collective-permute-start | bytes 393224 | tf_op jit(solution)/shard_map/ppermute | solution.py:26
  160.3 3.2 %collective-permute-start.31 = (bf16[192,128]{1,0:T(8,128)(2,1)}, bf16[192,128]{1,0:T(8,128)(2,1)S(1)}, u32[]{:S(2)}, u32[]{:S(2)}) collective-permute-start(bf16[192,128]{1,0:T(8,128)(2,1)} %get-tuple-element.59.b0), channel_id=1, source_target_pairs={{0,12},{1,13},{2,14},{3,15},{4,0},{5,1},{6,2},{7,3},{8,4},{9,5},{1... | collective-permute-start | bytes 147464 | tf_op jit(solution)/shard_map/ppermute | solution.py:26
  (118 shorter events, 48.0 us)
Async XLA Ops:
  4.6 16.1 %collective-permute-start.10 = (bf16[512,256]{1,0:T(8,128)(2,1)}, bf16[512,256]{1,0:T(8,128)(2,1)S(1)}, u32[]{:S(2)}, u32[]{:S(2)}) collective-permute-start(bf16[512,256]{1,0:T(8,128)(2,1)} %get-tuple-element.32.refs_4_), channel_id=1, source_target_pairs={{0,12},{1,13},{2,14},{3,15},{4,0},{5,1},{6,2},{7,3},{8,4},{9,5},{1... | collective-permute-start | bytes 786440 | tf_op jit(solution)/shard_map/ppermute | solution.py:26
  6.2 15.3 %collective-permute-start.11 = (bf16[512,256]{1,0:T(8,128)(2,1)}, bf16[512,256]{1,0:T(8,128)(2,1)S(1)}, u32[]{:S(2)}, u32[]{:S(2)}) collective-permute-start(bf16[512,256]{1,0:T(8,128)(2,1)} %get-tuple-element.32.refs_4_), channel_id=1, source_target_pairs={{0,8},{1,9},{2,10},{3,11},{4,12},{5,13},{6,14},{7,15},{8,0},{9,1},... | collective-permute-start | bytes 786440 | tf_op jit(solution)/shard_map/ppermute | solution.py:26
  13.8 26.5 %collective-permute-start.8 = (bf16[1024,256]{1,0:T(8,128)(2,1)}, bf16[1024,256]{1,0:T(8,128)(2,1)S(1)}, u32[]{:S(2)}, u32[]{:S(2)}) collective-permute-start(bf16[1024,256]{1,0:T(8,128)(2,1)} %constant_dynamic-update-slice_fusion.4), channel_id=1, source_target_pairs={{0,1},{1,2},{2,3},{3,0},{4,5},{5,6},{6,7},{7,4},{8,9},{9,10},{10,1... | collective-permute-start | bytes 1572872 | tf_op jit(solution)/shard_map/ppermute | solution.py:26
  17.9 22.5 %collective-permute-start.1 = (bf16[1024,256]{1,0:T(8,128)(2,1)}, bf16[1024,256]{1,0:T(8,128)(2,1)S(1)}, u32[]{:S(2)}, u32[]{:S(2)}) collective-permute-start(bf16[1024,256]{1,0:T(8,128)(2,1)} %constant_dynamic-update-slice_fusion), channel_id=1, source_target_pairs={{0,4},{1,5},{2,6},{3,7},{4,8},{5,9},{6,10},{7,11},{8,12},{9,13},{1... | collective-permute-start | bytes 1572872 | tf_op jit(solution)/shard_map/ppermute | solution.py:26
  20.7 15.9 %collective-permute-start.4 = (bf16[512,256]{1,0:T(8,128)(2,1)}, bf16[512,256]{1,0:T(8,128)(2,1)S(1)}, u32[]{:S(2)}, u32[]{:S(2)}) collective-permute-start(bf16[512,256]{1,0:T(8,128)(2,1)} %get-tuple-element.31.refs_0_), channel_id=1, source_target_pairs={{0,2},{1,3},{2,0},{3,1},{4,6},{5,7},{6,4},{7,5},{8,10},{9,11},{10,... | collective-permute-start | bytes 786440 | tf_op jit(solution)/shard_map/ppermute | solution.py:26
  21.5 23.2 %collective-permute-start.17 = (bf16[1024,256]{1,0:T(8,128)(2,1)}, bf16[1024,256]{1,0:T(8,128)(2,1)S(1)}, u32[]{:S(2)}, u32[]{:S(2)}) collective-permute-start(bf16[1024,256]{1,0:T(8,128)(2,1)} %constant_dynamic-update-slice_fusion.4), channel_id=1, source_target_pairs={{0,3},{1,0},{2,1},{3,2},{4,7},{5,4},{6,5},{7,6},{8,11},{9,8},{10,9... | collective-permute-start | bytes 1572872 | tf_op jit(solution)/shard_map/ppermute | solution.py:26
  31.7 24.9 %collective-permute-start.12 = (bf16[1024,256]{1,0:T(8,128)(2,1)}, bf16[1024,256]{1,0:T(8,128)(2,1)S(1)}, u32[]{:S(2)}, u32[]{:S(2)}) collective-permute-start(bf16[1024,256]{1,0:T(8,128)(2,1)} %constant_dynamic-update-slice_fusion.6), channel_id=1, source_target_pairs={{0,3},{1,0},{2,1},{3,2},{4,7},{5,4},{6,5},{7,6},{8,11},{9,8},{10,9... | collective-permute-start | bytes 1572872 | tf_op jit(solution)/shard_map/ppermute | solution.py:26
  38.0 21.8 %collective-permute-start.5 = (bf16[1024,256]{1,0:T(8,128)(2,1)}, bf16[1024,256]{1,0:T(8,128)(2,1)S(1)}, u32[]{:S(2)}, u32[]{:S(2)}) collective-permute-start(bf16[1024,256]{1,0:T(8,128)(2,1)} %constant_dynamic-update-slice_fusion.2), channel_id=1, source_target_pairs={{0,12},{1,13},{2,14},{3,15},{4,0},{5,1},{6,2},{7,3},{8,4},{9,5},{1... | collective-permute-start | bytes 1572872 | tf_op jit(solution)/shard_map/ppermute | solution.py:26
  40.3 24.0 %collective-permute-start.16 = (bf16[1024,256]{1,0:T(8,128)(2,1)}, bf16[1024,256]{1,0:T(8,128)(2,1)}, u32[]{:S(2)}, u32[]{:S(2)}) collective-permute-start(bf16[1024,256]{1,0:T(8,128)(2,1)} %constant_dynamic-update-slice_fusion), channel_id=1, source_target_pairs={{0,12},{1,13},{2,14},{3,15},{4,0},{5,1},{6,2},{7,3},{8,4},{9,5},{1... | collective-permute-start | bytes 1572872 | tf_op jit(solution)/shard_map/ppermute | solution.py:26
  40.4 23.9 %collective-permute-start.14 = (bf16[1024,256]{1,0:T(8,128)(2,1)}, bf16[1024,256]{1,0:T(8,128)(2,1)S(1)}, u32[]{:S(2)}, u32[]{:S(2)}) collective-permute-start(bf16[1024,256]{1,0:T(8,128)(2,1)} %constant_dynamic-update-slice_fusion.2), channel_id=1, source_target_pairs={{0,4},{1,5},{2,6},{3,7},{4,8},{5,9},{6,10},{7,11},{8,12},{9,13},{1... | collective-permute-start | bytes 1572872 | tf_op jit(solution)/shard_map/ppermute | solution.py:26
  44.7 32.4 %collective-permute-start.15 = (bf16[1024,256]{1,0:T(8,128)(2,1)}, bf16[1024,256]{1,0:T(8,128)(2,1)}, u32[]{:S(2)}, u32[]{:S(2)}) collective-permute-start(bf16[1024,256]{1,0:T(8,128)(2,1)} %constant_dynamic-update-slice_fusion.6), channel_id=1, source_target_pairs={{0,1},{1,2},{2,3},{3,0},{4,5},{5,6},{6,7},{7,4},{8,9},{9,10},{10,1... | collective-permute-start | bytes 1572872 | tf_op jit(solution)/shard_map/ppermute | solution.py:26
  56.6 33.0 %collective-permute-start.13 = (bf16[1024,256]{1,0:T(8,128)(2,1)S(1)}, bf16[1024,256]{1,0:T(8,128)(2,1)S(1)}, u32[]{:S(2)}, u32[]{:S(2)}) collective-permute-start(bf16[1024,256]{1,0:T(8,128)(2,1)S(1)} %collective-permute-done.12.refs_6_.refs_7_), channel_id=1, source_target_pairs={{0,3},{1,0},{2,1},{3,2},{4,7},{5,4},{6,5},{7,6},{8,11},{9,8},{10,9... | collective-permute-start | bytes 1572872 | tf_op jit(solution)/shard_map/ppermute | solution.py:26
  59.7 29.9 %collective-permute-start.6 = (bf16[1024,256]{1,0:T(8,128)(2,1)S(1)}, bf16[1024,256]{1,0:T(8,128)(2,1)}, u32[]{:S(2)}, u32[]{:S(2)}) collective-permute-start(bf16[1024,256]{1,0:T(8,128)(2,1)S(1)} %collective-permute-done.5.refs_2_.refs_3_), channel_id=1, source_target_pairs={{0,12},{1,13},{2,14},{3,15},{4,0},{5,1},{6,2},{7,3},{8,4},{9,5},{1... | collective-permute-start | bytes 1572872 | tf_op jit(solution)/shard_map/ppermute | solution.py:26
  64.3 25.3 %collective-permute-start.9 = (bf16[1024,256]{1,0:T(8,128)(2,1)S(1)}, bf16[1024,256]{1,0:T(8,128)(2,1)}, u32[]{:S(2)}, u32[]{:S(2)}) collective-permute-start(bf16[1024,256]{1,0:T(8,128)(2,1)S(1)} %collective-permute-done.8.refs_4_.refs_5_), channel_id=1, source_target_pairs={{0,1},{1,2},{2,3},{3,0},{4,5},{5,6},{6,7},{7,4},{8,9},{9,10},{10,1... | collective-permute-start | bytes 1572872 | tf_op jit(solution)/shard_map/ppermute | solution.py:26
  64.4 25.3 %collective-permute-start.2 = (bf16[1024,256]{1,0:T(8,128)(2,1)S(1)}, bf16[1024,256]{1,0:T(8,128)(2,1)}, u32[]{:S(2)}, u32[]{:S(2)}) collective-permute-start(bf16[1024,256]{1,0:T(8,128)(2,1)S(1)} %collective-permute-done.1.refs_0_.refs_1_), channel_id=1, source_target_pairs={{0,4},{1,5},{2,6},{3,7},{4,8},{5,9},{6,10},{7,11},{8,12},{9,13},{1... | collective-permute-start | bytes 1572872 | tf_op jit(solution)/shard_map/ppermute | solution.py:26
  114.4 16.3 %collective-permute-start.18 = (bf16[128,2304]{1,0:T(8,128)(2,1)}, bf16[128,2304]{1,0:T(8,128)(2,1)S(1)}, u32[]{:S(2)}, u32[]{:S(2)}) collective-permute-start(bf16[128,2304]{1,0:T(8,128)(2,1)} %get-tuple-element.43), channel_id=1, source_target_pairs={{0,4},{1,5},{2,6},{3,7},{4,8},{5,9},{6,10},{7,11},{8,12},{9,13},{1... | collective-permute-start | bytes 1769480 | tf_op jit(solution)/shard_map/ppermute | solution.py:26
  114.4 20.3 %collective-permute-start.19 = (bf16[128,2304]{1,0:T(8,128)(2,1)}, bf16[128,2304]{1,0:T(8,128)(2,1)S(1)}, u32[]{:S(2)}, u32[]{:S(2)}) collective-permute-start(bf16[128,2304]{1,0:T(8,128)(2,1)} %get-tuple-element.44), channel_id=1, source_target_pairs={{0,12},{1,13},{2,14},{3,15},{4,0},{5,1},{6,2},{7,3},{8,4},{9,5},{1... | collective-permute-start | bytes 1769480 | tf_op jit(solution)/shard_map/ppermute | solution.py:26
  117.6 18.8 %collective-permute-start.20 = (bf16[128,2304]{1,0:T(8,128)(2,1)}, bf16[128,2304]{1,0:T(8,128)(2,1)S(1)}, u32[]{:S(2)}, u32[]{:S(2)}) collective-permute-start(bf16[128,2304]{1,0:T(8,128)(2,1)} %get-tuple-element.45), channel_id=1, source_target_pairs={{0,8},{1,9},{2,10},{3,11},{4,12},{5,13},{6,14},{7,15},{8,0},{9,1},... | collective-permute-start | bytes 1769480 | tf_op jit(solution)/shard_map/ppermute | solution.py:26
  127.4 16.7 %collective-permute-start.24 = (bf16[128,2048]{1,0:T(8,128)(2,1)}, bf16[128,2048]{1,0:T(8,128)(2,1)S(1)}, u32[]{:S(2)}, u32[]{:S(2)}) collective-permute-start(bf16[128,2048]{1,0:T(8,128)(2,1)} %get-tuple-element.52), channel_id=1, source_target_pairs={{0,1},{1,2},{2,3},{3,0},{4,5},{5,6},{6,7},{7,4},{8,9},{9,10},{10,1... | collective-permute-start | bytes 1572872 | tf_op jit(solution)/shard_map/ppermute | solution.py:26
  127.4 21.0 %collective-permute-start.25 = (bf16[128,2048]{1,0:T(8,128)(2,1)}, bf16[128,2048]{1,0:T(8,128)(2,1)S(1)}, u32[]{:S(2)}, u32[]{:S(2)}) collective-permute-start(bf16[128,2048]{1,0:T(8,128)(2,1)} %get-tuple-element.53), channel_id=1, source_target_pairs={{0,3},{1,0},{2,1},{3,2},{4,7},{5,4},{6,5},{7,6},{8,11},{9,8},{10,9... | collective-permute-start | bytes 1572872 | tf_op jit(solution)/shard_map/ppermute | solution.py:26
  130.6 19.2 %collective-permute-start.26 = (bf16[128,2048]{1,0:T(8,128)(2,1)}, bf16[128,2048]{1,0:T(8,128)(2,1)S(1)}, u32[]{:S(2)}, u32[]{:S(2)}) collective-permute-start(bf16[128,2048]{1,0:T(8,128)(2,1)} %get-tuple-element.54), channel_id=1, source_target_pairs={{0,2},{1,3},{2,0},{3,1},{4,6},{5,7},{6,4},{7,5},{8,10},{9,11},{10,... | collective-permute-start | bytes 1572872 | tf_op jit(solution)/shard_map/ppermute | solution.py:26
  140.2 16.4 %collective-permute-start.21 = (bf16[32,2816]{1,0:T(8,128)(2,1)}, bf16[32,2816]{1,0:T(8,128)(2,1)S(1)}, u32[]{:S(2)}, u32[]{:S(2)}) collective-permute-start(bf16[32,2816]{1,0:T(8,128)(2,1)} %get-tuple-element.47), channel_id=1, source_target_pairs={{0,1},{1,2},{2,3},{3,0},{4,5},{5,6},{6,7},{7,4},{8,9},{9,10},{10,1... | collective-permute-start | bytes 540680 | tf_op jit(solution)/shard_map/ppermute | solution.py:26
  141.5 16.0 %collective-permute-start.22 = (bf16[32,2816]{1,0:T(8,128)(2,1)}, bf16[32,2816]{1,0:T(8,128)(2,1)S(1)}, u32[]{:S(2)}, u32[]{:S(2)}) collective-permute-start(bf16[32,2816]{1,0:T(8,128)(2,1)} %get-tuple-element.48), channel_id=1, source_target_pairs={{0,3},{1,0},{2,1},{3,2},{4,7},{5,4},{6,5},{7,6},{8,11},{9,8},{10,9... | collective-permute-start | bytes 540680 | tf_op jit(solution)/shard_map/ppermute | solution.py:26
  144.1 13.5 %collective-permute-start.23 = (bf16[32,2816]{1,0:T(8,128)(2,1)}, bf16[32,2816]{1,0:T(8,128)(2,1)S(1)}, u32[]{:S(2)}, u32[]{:S(2)}) collective-permute-start(bf16[32,2816]{1,0:T(8,128)(2,1)} %get-tuple-element.49), channel_id=1, source_target_pairs={{0,2},{1,3},{2,0},{3,1},{4,6},{5,7},{6,4},{7,5},{8,10},{9,11},{10,... | collective-permute-start | bytes 540680 | tf_op jit(solution)/shard_map/ppermute | solution.py:26
  (37 other events, 301.9 us)
